TPU v7x, 512 devices: a whole 4x4x16 slice. The times are simulated.
512 devices in a mesh: grp: 32 (over y, x, core), tp: 16 (over z).
Axes of the slice: x: 4, y: 4, z: 16, core: 2. Of those that a mesh axis runs over, the one named last changes fastest.
Arguments:
- trainer_increment: float32 [1024, 128, 128], P(('tp', 'grp')), may hold values from -0.3125 to 0.3125
- trainer_residual: float32 [1024, 128, 128], P(('tp', 'grp')), may hold values from -0.3125 to 0.3125
- partition_tile_indices: int32 [512, 2], P(('tp', 'grp')), may hold values from 0 to 1, as said below
- retained_tallies: int32 [512], P(('tp', 'grp')), may hold values from 0 to 2, as said below
- projection_parameters: bfloat16 [8192, 2048], P('tp'), may hold values from -0.0625 to 0.0625
- normalized_activations: bfloat16 [4, 32, 8192], P(None, 'grp', 'tp'), may hold values from -6 to 6
- rotated_questions: bfloat16 [4, 32, 8192], P(None, 'grp'), may hold values from -256 to 256
- stored_attention_memory: bfloat16 [32, 8192, 2048], P('grp', 'tp'), may hold values from -6 to 6
- memory_fill_lengths: int32 [32], P('grp'), may hold values from 2 to 8192, as said below
Outputs:
- new_error: float32 [1024, 128, 128], P(('tp', 'grp'))
- new_kv: bfloat16 [4, 32, 2048], P(None, 'grp', 'tp')
- attention: bfloat16 [4, 32, 8192], P(None, 'grp', 'tp')
Inputs may be any that keep to these rules, and one draw needn't show every extreme that they name: `partition_tile_indices`: each row lists the local block numbers of one shard, each once; only its first retained_tallies entries name surviving blocks. `retained_tallies`: some shard lists all 2 of its blocks in every draw. Row r's valid cache positions are 0 to memory_fill_lengths[r] - 1; some row has all 8192 in every draw.
All inputs are finite; a program needn't handle non-finite values.
Results may differ from a plain program's by a relative error of at most 0.02.
Values may be sent and summed in bfloat16 or wider, within the bound.
A program may use at most 64 MiB of HBM per device.

v0:
```python
import math
import jax
import jax.numpy as jnp
from jax import lax
from jax.sharding import PartitionSpec as P

HD = 128
BLK = 128
NEG = -1e30


def merged(array, axis, combine):
    everything = jax.tree.map(lambda part: lax.all_gather(part, axis), array)
    initial = jax.tree.map(lambda part: part[0], everything)

    def step(k, so_far):
        return combine(so_far, jax.tree.map(lambda part: part[k], everything))

    return lax.fori_loop(1, lax.axis_size(axis), step, initial)


def retained_tiles(partition_tile_indices, retained_tallies):
    slots = partition_tile_indices.shape[1]
    sorting_permutation = jnp.arange(slots, dtype=jnp.int32)
    enumerated_tiles = sorting_permutation[None, :] < retained_tallies[:, None]
    hits = (
        partition_tile_indices[:, :, None] == sorting_permutation[None, None, :]
    ) & enumerated_tiles[:, :, None]
    return jnp.any(hits, axis=1)


def combine(first, second):
    top_a, total_a, blended_first = first
    top_b, total_b, mixed_b = second
    top = jnp.maximum(top_a, top_b)
    scale_a = jnp.exp(top_a - top)
    scale_b = jnp.exp(top_b - top)
    total = total_a * scale_a + total_b * scale_b
    mixed = blended_first * scale_a[..., None] + mixed_b * scale_b[..., None]
    return (top, total, mixed)


def cache_partial(rotated_questions, stored_attention_memory, memory_fill_lengths, first):
    steps, rows, width = rotated_questions.shape
    span = stored_attention_memory.shape[1]
    heads_kv = stored_attention_memory.shape[2] // (2 * HD)
    group = width // HD // heads_kv
    scale = 1.0 / math.sqrt(HD)
    query = rotated_questions.reshape(steps, rows, heads_kv, group, HD)
    cache_rows_held = stored_attention_memory.reshape(rows, span, heads_kv, 2, HD)
    scores = (
        jnp.einsum(
            "srhgd,rphd->srhgp",
            query,
            cache_rows_held[:, :, :, 0],
            preferred_element_type=jnp.float32,
        )
        * scale
    )
    position = first + jnp.arange(span, dtype=jnp.int32)
    valid = (position[None, :] < memory_fill_lengths[:, None])[None, :, None, None, :]
    scores = jnp.where(valid, scores, NEG)
    top = jnp.max(scores, axis=-1)
    probs = jnp.where(valid, jnp.exp(scores - top[..., None]), 0.0)
    total = jnp.sum(probs, axis=-1)
    values = cache_rows_held[:, :, :, 1].astype(jnp.float32)
    mixed = jnp.einsum("srhgp,rphd->srhgd", probs, values, precision=lax.Precision.HIGHEST)
    heads = heads_kv * group
    return (
        top.reshape(steps, rows, heads),
        total.reshape(steps, rows, heads),
        mixed.reshape(steps, rows, heads, HD),
    )


def body(
    trainer_increment,
    trainer_residual,
    partition_tile_indices,
    retained_tallies,
    projection_parameters,
    normalized_activations,
    rotated_questions,
    stored_attention_memory,
    memory_fill_lengths,
):
    summed = trainer_increment + trainer_residual
    retain_markers = retained_tiles(partition_tile_indices, retained_tallies).reshape(-1)
    sent = jnp.where(
        retain_markers[:, None, None], summed.astype(jnp.bfloat16), jnp.zeros((), jnp.bfloat16)
    )
    new_error = summed - sent.astype(jnp.float32)
    blocks = lax.all_gather(sent, "grp", axis=0, tiled=True)
    local_feats, kvw = projection_parameters.shape
    update = (
        blocks.reshape(local_feats // BLK, kvw // BLK, BLK, BLK)
        .transpose(0, 2, 1, 3)
        .reshape(local_feats, kvw)
    )
    patched = (projection_parameters.astype(jnp.float32) + update.astype(jnp.float32)).astype(
        jnp.bfloat16
    )
    steps, local_rows, width = normalized_activations.shape
    partial_kv = jnp.dot(
        normalized_activations.reshape(steps * local_rows, width),
        patched,
        preferred_element_type=jnp.float32,
    )
    ranks = lax.axis_size("tp")
    rank = lax.axis_index("tp")
    columns = kvw // ranks
    kv_full = lax.psum(partial_kv, "tp").astype(jnp.bfloat16)
    kv_own = lax.dynamic_slice_in_dim(kv_full, rank * columns, columns, 1)
    new_kv = kv_own.reshape(steps, local_rows, columns)
    span = stored_attention_memory.shape[1]
    top, total, mixed = cache_partial(
        rotated_questions, stored_attention_memory, memory_fill_lengths, rank * span
    )
    heads = top.shape[2]
    own = heads // ranks
    top, total, mixed = merged((top, total, mixed), "tp", combine)
    top = lax.dynamic_slice_in_dim(top, rank * own, own, 2)
    total = lax.dynamic_slice_in_dim(total, rank * own, own, 2)
    mixed = lax.dynamic_slice_in_dim(mixed, rank * own, own, 2)
    heads_kv = kvw // (2 * HD)
    group = heads // heads_kv
    scale = 1.0 / math.sqrt(HD)
    fresh = kv_full.reshape(steps, local_rows, heads_kv, 2, HD)
    head_ids = (rank * own + jnp.arange(own, dtype=jnp.int32)) // group
    fresh = jnp.take(fresh, head_ids, axis=2)
    query = lax.dynamic_slice_in_dim(rotated_questions, rank * own * HD, own * HD, 2).reshape(
        steps, local_rows, own, HD
    )
    scores = (
        jnp.einsum("srjd,urjd->srju", query, fresh[:, :, :, 0], preferred_element_type=jnp.float32)
        * scale
    )
    step_ids = jnp.arange(steps, dtype=jnp.int32)
    causal = (step_ids[None, :] <= step_ids[:, None])[:, None, None, :]
    scores = jnp.where(causal, scores, NEG)
    peak = jnp.maximum(top, jnp.max(scores, axis=-1))
    probs = jnp.where(causal, jnp.exp(scores - peak[..., None]), 0.0)
    carried = jnp.exp(top - peak)
    denom = total * carried + jnp.sum(probs, axis=-1)
    values = fresh[:, :, :, 1].astype(jnp.float32)
    numer = mixed * carried[..., None] + jnp.einsum(
        "srju,urjd->srjd", probs, values, precision=lax.Precision.HIGHEST
    )
    attention = (numer / denom[..., None]).reshape(steps, local_rows, own * HD).astype(jnp.bfloat16)
    return (new_error, new_kv, attention)


def solution(mesh):
    placed = (
        P(("tp", "grp"), None, None),
        P(("tp", "grp"), None, None),
        P(("tp", "grp"), None),
        P(("tp", "grp")),
        P("tp", None),
        P(None, "grp", "tp"),
        P(None, "grp", None),
        P("grp", "tp", None),
        P("grp"),
    )
    return jax.shard_map(
        body,
        mesh=mesh,
        in_specs=placed,
        out_specs=(P(("tp", "grp"), None, None), P(None, "grp", "tp"), P(None, "grp", "tp")),
        check_vma=False,
    )
```

profile of v0, /device:TPU:2, one launch (start us, length us, event | category | flops | bytes accessed | tf_op | source)
XLA Modules:
  0.0 221.9 jit_solution(10214104289567611357)
XLA Ops:
  7.2 2.9 %copy.91 = bf16[1,512,2048]{1,2,0:T(8,128)(2,1)S(1)} copy(bf16[1,512,2048]{2,1,0:T(8,128)(2,1)} %param.18) | data formatting | bytes 4194304 | tf_op args[7]
  11.2 1.1 convolution_bitcast_fusion.1
  15.7 35.6 %all_gather.13 = f32[16,4,1,64]{3,1,2,0:T(4,128)S(1)} all-gather(f32[1,4,1,64]{3,1,2,0:T(4,128)S(1)} %all_gather_reshape.9), channel_id=1, replica_groups=mesh['grp'=32,'tp'=16] {'tp'}, dimensions={0}, use_global_device_ids=true | all-gather | bytes 17408 | tf_op jit(solution)/shard_map/all_gather | solution.py:13
  51.4 26.1 %all_gather.14 = f32[16,4,1,64]{3,1,2,0:T(4,128)S(1)} all-gather(f32[1,4,1,64]{3,1,2,0:T(4,128)S(1)} %all_gather_reshape.10), channel_id=1, replica_groups=mesh['grp'=32,'tp'=16] {'tp'}, dimensions={0}, use_global_device_ids=true | all-gather | bytes 17408 | tf_op jit(solution)/shard_map/all_gather | solution.py:13
  77.5 13.1 %all-gather.5.cloned.1.call-done = f32[16,4,1,64,128]{4,3,2,1,0:T(8,128)} async-done(((f32[1,4,1,64,128]{4,3,2,1,0:T(8,128)}), f32[16,4,1,64,128]{4,3,2,1,0:T(8,128)}) %all-gather.5.cloned.1.call-update) | async-done | bytes 2097168 | tf_op jit(solution)/shard_map/all_gather | solution.py:13
  91.5 17.1 %while.19 = (s32[]{:T(128)}, f32[4,1,64]{2,1,0:T(1,128)S(1)}, f32[4,1,64]{2,1,0:T(1,128)S(1)}, f32[4,1,64,128]{3,2,1,0:T(8,128)S(1)}, f32[16,4,1,64]{3,1,2,0:T(4...) while((s32[]{:T(128)}, f32[4,1,64]{2,1,0:T(1,128)S(1)}, ...), condition=%wide.region_5.6_spmd, body=%wide.region_4.5_spmd.sunk | while | flops 99845 | bytes 407703 | solution.py:19
  91.5 1.1 fusion.37
  92.7 1.1 fusion.37
  93.8 1.1 fusion.37
  94.9 1.1 fusion.37
  96.1 1.1 fusion.37
  97.2 1.1 fusion.37
  98.4 1.1 fusion.37
  99.5 1.1 fusion.37
  100.6 1.1 fusion.37
  101.8 1.1 fusion.37
  102.9 1.1 fusion.37
  104.1 1.1 fusion.37
  107.5 1.1 fusion.37
  108.7 40.8 %all-gather.3.cloned.1.call-done = bf16[64,128,128]{2,1,0:T(8,128)(2,1)} async-done(((bf16[2,128,128]{2,1,0:T(8,128)(2,1)}), bf16[64,128,128]{2,1,0:T(8,128)(2,1)}) %all-gather.3.cloned.1.call-update) | async-done | bytes 2097168 | tf_op jit(solution)/shard_map/all_gather | solution.py:93
  149.5 2.1 convert_bitcast_fusion
  151.6 2.4 %copy.90 = f32[4,128,16,128]{3,2,1,0:T(8,128)S(1)} copy(f32[4,128,16,128]{3,1,2,0:T(8,128)S(1)} %convert_bitcast_fusion) | data formatting | bytes 8388608 | tf_op jit(solution)/shard_map/convert_element_type | solution.py:100
  154.1 1.3 convolution_bitcast_fusion
  155.4 56.9 %psum.7 = bf16[4,2048]{1,0:T(4,128)(2,1)S(1)} all-reduce(f32[4,2048]{1,0:T(4,128)S(1)} %convolution_bitcast_fusion), channel_id=1, replica_groups=mesh['grp'=32,'tp'=16] {'tp'}, use_global_device_ids=true, to_apply=%region_1.2 | all-reduce | flops 8192 | bytes 49152 | tf_op jit(solution)/shard_map/psum | solution.py:112
  (81 shorter events, 9.7 us)
Async XLA Ops:
  7.2 146.9 %copy-start = (bf16[4,1,512]{2,0,1:T(4,128)(2,1)S(1)}, bf16[4,1,512]{2,0,1:T(4,128)(2,1)}, u32[]{:S(2)}) copy-start(bf16[4,1,512]{2,0,1:T(4,128)(2,1)} %param.16) | copy-start | bytes 12292
  7.2 83.4 %all-gather.5.cloned.1.call-start = ((), (), s32[]{:S(2)}) async-start(), calls=%async_computation.1 | async-start | bytes 2228224 | tf_op jit(solution)/shard_map/all_gather | solution.py:13
  7.2 3.6 %copy-start.4 = (bf16[4,1,8192]{2,0,1:T(4,128)(2,1)S(1)}, bf16[4,1,8192]{2,0,1:T(4,128)(2,1)}, u32[]{:S(2)}) copy-start(bf16[4,1,8192]{2,0,1:T(4,128)(2,1)} %param.17) | copy-start | bytes 196612
  10.8 3.0 %copy-start.5 = (s32[1,2]{1,0:T(1,128)S(1)}, s32[1,2]{1,0:T(1,128)}, u32[]{:S(2)}) copy-start(s32[1,2]{1,0:T(1,128)} %param.13) | copy-start | bytes 28
  10.8 3.0 %copy-start.2 = (f32[2,128,128]{2,1,0:T(8,128)S(1)}, f32[2,128,128]{2,1,0:T(8,128)}, u32[]{:S(2)}) copy-start(f32[2,128,128]{2,1,0:T(8,128)} %param.11) | copy-start | bytes 393220
  10.8 3.0 %copy-start.3 = (f32[2,128,128]{2,1,0:T(8,128)S(1)}, f32[2,128,128]{2,1,0:T(8,128)}, u32[]{:S(2)}) copy-start(f32[2,128,128]{2,1,0:T(8,128)} %param.12) | copy-start | bytes 393220
  13.1 136.4 %all-gather.3.cloned.1.call-start = ((), (), s32[]{:S(2)}) async-start(), calls=%async_computation | async-start | bytes 2162688 | tf_op jit(solution)/shard_map/all_gather | solution.py:93
  151.6 2.5 %copy-start.1 = (bf16[512,2048]{1,0:T(8,128)(2,1)S(1)}, bf16[512,2048]{1,0:T(8,128)(2,1)}, u32[]{:S(2)}) copy-start(bf16[512,2048]{1,0:T(8,128)(2,1)} %param.15) | copy-start | bytes 6291460
Sparse Core Ops, SparseCore 0:
  13.2 77.3 all-gather.4
  93.7 55.7 all-gather.2
where the time goes:
time: 222 us
  blocking collectives  119 us (54%)
  waiting for transfers between devices  53.9 us (24%)
  other arithmetic  20.7 us (9%)
  between operations  15.5 us (7%)
  local copies, waits for them, and re-layouts  8.93 us (4%)
  matrix products  3.81 us (2%)
    all_gather x2, blocking collectives, merged(): everything = jax.tree.map(lambda part: lax.all_gather(part, axis), array)  61.6 us
    psum x1, blocking collectives, body(): kv_full = lax.psum(partial_kv, 'tp').astype(jnp.bfloat16)  56.9 us
    all_gather x1, waiting for transfers between devices, body(): blocks = lax.all_gather(sent, 'grp', axis=0, tiled=True)  40.8 us
    add x15, other arithmetic, combine(): mixed = blended_first * scale_a[..., None] + mixed_b * scale_b[..., None]  16.1 us
    all_gather x1, waiting for transfers between devices, merged(): everything = jax.tree.map(lambda part: lax.all_gather(part, axis), array)  13.1 us
  transfers between devices with their start and end apart: 2, of which 2 were waited for; matrix products, arithmetic and copies ran while one was open for 9% of the time, Pallas kernels for 0%

commit v1 on v0

--- a/solution.py
+++ b/solution.py
@@ -90,7 +90,9 @@
         retain_markers[:, None, None], summed.astype(jnp.bfloat16), jnp.zeros((), jnp.bfloat16)
     )
     new_error = summed - sent.astype(jnp.float32)
-    blocks = lax.all_gather(sent, "grp", axis=0, tiled=True)
+    blocks = jnp.concatenate(
+        lax.all_to_all(jnp.stack(lax.psum(1, "grp") * [sent]), "grp", 0, 0), axis=0
+    )
     local_feats, kvw = projection_parameters.shape
     update = (
         blocks.reshape(local_feats // BLK, kvw // BLK, BLK, BLK)

time: 222 us -> 174 us (0.78)
  waiting for transfers between devices: 53.9 us -> 0.02 us
  starting transfers between devices: 0.08 us -> 9.59 us
  blocking collectives: 119 us -> 114 us
    all_gather x1 -> x0, waiting for transfers between devices: 40.8 us -> none  [body(): blocks = lax.all_gather(sent, 'grp', axis=0, tiled=True)]
    all_gather x1, waiting for transfers between devices: 13.1 us -> 0.01 us  [merged(): everything = jax.tree.map(lambda part: lax.all_gather(part, axis), array)]
    all_to_all x0 -> x1, starting transfers between devices: none -> 9.55 us  [body(): lax.all_to_all(jnp.stack(lax.psum(1, 'grp') * [sent]), 'grp', 0, 0)]
    psum x1, blocking collectives: 56.9 us -> 54.5 us  [body(): kv_full = lax.psum(partial_kv, 'tp').astype(jnp.bfloat16)]
  transfers between devices with their start and end apart: 2 -> 2, of which waited for: 2 -> 0; matrix products, arithmetic and copies ran while one was open for 9% -> 5% of each run, Pallas kernels for 0% -> 0%
where the time goes in v1:
time: 174 us; the launch traced here: 173 us
  blocking collectives  114 us (66%)
  other arithmetic  18.5 us (11%)
  between operations  15.5 us (9%)
  local copies, waits for them, and re-layouts  10.7 us (6%)
  starting transfers between devices  9.59 us (6%)
  matrix products  3.81 us (2%)
    all_gather x2, blocking collectives, merged(): everything = jax.tree.map(lambda part: lax.all_gather(part, axis), array)  59.8 us
    psum x1, blocking collectives, body(): kv_full = lax.psum(partial_kv, 'tp').astype(jnp.bfloat16)  54.5 us
    add x15, other arithmetic, combine(): mixed = blended_first * scale_a[..., None] + mixed_b * scale_b[..., None]  16.1 us
    all_to_all x1, starting transfers between devices, body(): lax.all_to_all(jnp.stack(lax.psum(1, 'grp') * [sent]), 'grp', 0, 0)  9.55 us
  transfers between devices with their start and end apart: 2, of which 0 were waited for; matrix products, arithmetic and copies ran while one was open for 5% of the time, Pallas kernels for 0%

profile of v1, /device:TPU:2, one launch (start us, length us, event | category | flops | bytes accessed | tf_op | source)
XLA Modules:
  0.0 172.9 jit_solution(15371678002931211246)
XLA Ops:
  7.2 2.9 %copy.107 = bf16[1,512,2048]{1,2,0:T(8,128)(2,1)S(1)} copy(bf16[1,512,2048]{2,1,0:T(8,128)(2,1)} %param.18) | data formatting | bytes 4194304 | tf_op args[7]
  11.2 1.2 convolution_bitcast_fusion.1
  13.9 1.8 %stack.2 = bf16[32,2,128,128]{3,2,1,0:T(8,128)(2,1)} broadcast(bf16[2,128,128]{2,1,0:T(8,128)(2,1)S(1)} %convert_select_fusion), dimensions={1,2,3} | broadcast | bytes 2162688 | tf_op jit(solution)/shard_map/stack | solution.py:94
  15.7 9.5 %all-to-all-start = ((bf16[32,2,128,128]{3,2,1,0:T(8,128)(2,1)}), bf16[32,2,128,128]{3,2,1,0:T(8,128)(2,1)S(1)}, u32[]{:S(2)}, u32[]{:S(2)}) async-start(bf16[32,2,128,128]{3,2,1,0:T(8,128)(2,1)} %stack.2), calls=%async_computation | async-start | bytes 4194304 | tf_op jit(solution)/shard_map/all_to_all | solution.py:94
  25.4 33.6 %all_gather.9 = f32[16,4,1,64]{3,1,2,0:T(4,128)S(1)} all-gather(f32[1,4,1,64]{3,1,2,0:T(4,128)S(1)} %all_gather_reshape.9), channel_id=1, replica_groups=mesh['grp'=32,'tp'=16] {'tp'}, dimensions={0}, use_global_device_ids=true | all-gather | bytes 17408 | tf_op jit(solution)/shard_map/all_gather | solution.py:13
  59.3 26.1 %all_gather.10 = f32[16,4,1,64]{3,1,2,0:T(4,128)S(1)} all-gather(f32[1,4,1,64]{3,1,2,0:T(4,128)S(1)} %all_gather_reshape.10), channel_id=1, replica_groups=mesh['grp'=32,'tp'=16] {'tp'}, dimensions={0}, use_global_device_ids=true | all-gather | bytes 17408 | tf_op jit(solution)/shard_map/all_gather | solution.py:13
  86.8 2.4 %copy.106 = f32[4,128,16,128]{3,2,1,0:T(8,128)S(1)} copy(f32[4,128,16,128]{3,1,2,0:T(8,128)S(1)} %convert_bitcast_fusion) | data formatting | bytes 8388608 | tf_op jit(solution)/shard_map/convert_element_type | solution.py:102
  89.2 1.3 convolution_bitcast_fusion
  90.6 54.5 %psum.7 = bf16[4,2048]{1,0:T(4,128)(2,1)S(1)} all-reduce(f32[4,2048]{1,0:T(4,128)S(1)} %convolution_bitcast_fusion), channel_id=1, replica_groups=mesh['grp'=32,'tp'=16] {'tp'}, use_global_device_ids=true, to_apply=%region_1.2 | all-reduce | flops 8192 | bytes 49152 | tf_op jit(solution)/shard_map/psum | solution.py:114
  147.5 17.1 %while.19 = (s32[]{:T(128)}, f32[4,1,64]{2,1,0:T(1,128)S(1)}, f32[4,1,64]{2,1,0:T(1,128)S(1)}, f32[4,1,64,128]{3,2,1,0:T(8,128)S(1)}, f32[16,4,1,64]{3,1,2,0:T(4...) while((s32[]{:T(128)}, f32[4,1,64]{2,1,0:T(1,128)S(1)}, ...), condition=%wide.region_5.6_spmd, body=%wide.region_4.5_spmd.sunk | while | flops 99845 | bytes 407703 | solution.py:19
  147.6 1.1 fusion.37
  148.7 1.1 fusion.37
  149.8 1.1 fusion.37
  151.0 1.1 fusion.37
  152.1 1.1 fusion.37
  153.3 1.1 fusion.37
  154.4 1.1 fusion.37
  155.5 1.1 fusion.37
  156.7 1.1 fusion.37
  157.8 1.1 fusion.37
  159.0 1.1 fusion.37
  160.1 1.1 fusion.37
  161.2 1.1 fusion.37
  163.5 1.1 fusion.37
  (81 shorter events, 8.4 us)
Async XLA Ops:
  7.2 82.1 %copy-start = (bf16[4,1,512]{2,0,1:T(4,128)(2,1)S(1)}, bf16[4,1,512]{2,0,1:T(4,128)(2,1)}, u32[]{:S(2)}) copy-start(bf16[4,1,512]{2,0,1:T(4,128)(2,1)} %param.16) | copy-start | bytes 12292
  7.2 139.4 %all-gather.2.cloned.1.call-start = ((), (), s32[]{:S(2)}) async-start(), calls=%async_computation.1 | async-start | bytes 2228224 | tf_op jit(solution)/shard_map/all_gather | solution.py:13
  7.2 3.6 %copy-start.4 = (bf16[4,1,8192]{2,0,1:T(4,128)(2,1)S(1)}, bf16[4,1,8192]{2,0,1:T(4,128)(2,1)}, u32[]{:S(2)}) copy-start(bf16[4,1,8192]{2,0,1:T(4,128)(2,1)} %param.17) | copy-start | bytes 196612
  10.8 2.9 %copy-start.5 = (s32[1,2]{1,0:T(1,128)S(1)}, s32[1,2]{1,0:T(1,128)}, u32[]{:S(2)}) copy-start(s32[1,2]{1,0:T(1,128)} %param.13) | copy-start | bytes 28
  10.8 3.0 %copy-start.2 = (f32[2,128,128]{2,1,0:T(8,128)S(1)}, f32[2,128,128]{2,1,0:T(8,128)}, u32[]{:S(2)}) copy-start(f32[2,128,128]{2,1,0:T(8,128)} %param.11) | copy-start | bytes 393220
  10.8 3.0 %copy-start.3 = (f32[2,128,128]{2,1,0:T(8,128)S(1)}, f32[2,128,128]{2,1,0:T(8,128)}, u32[]{:S(2)}) copy-start(f32[2,128,128]{2,1,0:T(8,128)} %param.12) | copy-start | bytes 393220
  15.7 70.5 %all-to-all-start = ((bf16[32,2,128,128]{3,2,1,0:T(8,128)(2,1)}), bf16[32,2,128,128]{3,2,1,0:T(8,128)(2,1)S(1)}, u32[]{:S(2)}, u32[]{:S(2)}) async-start(bf16[32,2,128,128]{3,2,1,0:T(8,128)(2,1)} %stack.2), calls=%async_computation | async-start | bytes 4194304 | tf_op jit(solution)/shard_map/all_to_all | solution.py:94
  86.8 2.5 %copy-start.1 = (bf16[512,2048]{1,0:T(8,128)(2,1)S(1)}, bf16[512,2048]{1,0:T(8,128)(2,1)}, u32[]{:S(2)}) copy-start(bf16[512,2048]{1,0:T(8,128)(2,1)} %param.15) | copy-start | bytes 6291460
Sparse Core Ops, SparseCore 0:
  13.2 77.2 all-gather.1
